TPU v7x, 32 devices: a whole 2x2x4 slice. The times are simulated.
32 devices in a mesh: clip: 2 (over x), slab: 16 (over z, y, core).
Axes of the slice: x: 2, y: 2, z: 4, core: 2. Of those that a mesh axis runs over, the one named last changes fastest.
Arguments:
- mask_field: float32 [4096, 2048], P(('clip', 'slab')), parts along dimension 0, may hold values from -1.8 to 2.9
- target_print: int32 [4096, 2048], P(('clip', 'slab')), parts along dimension 0, may hold values from 0 to 1
- source_points: int32 [32, 2], P('clip'), parts along dimension 0, may hold values from 0 to 60
- source_groups: int32 [32], P('clip'), parts along dimension 0, may hold values from 0 to 7
- group_logits: float32 [16], P('clip'), parts along dimension 0, may hold values from -1 to 1
- pupil_radius: int32 [2], P('clip'), parts along dimension 0, may hold values from 32 to 127
Outputs:
- loss_value: float32 [2], P('clip'), parts along dimension 0
- mask_grad: float32 [4096, 2048], P(('clip', 'slab')), parts along dimension 0
- group_grad: float32 [16], P('clip'), parts along dimension 0
There are 2 independent parts, one for each index of `clip`. A program takes and returns all parts, laid end to end along the dimension named above; each array names one. Nothing has to cross between parts.
All inputs are finite; a program needn't handle non-finite values.
Results may differ from a plain program's by a relative error of at most 0.0003.
Values sent between devices are 32-bit elements; how exact they have to be, the bound alone decides.
A program may use at most 128 MiB of HBM per device.

v0:
```python
import functools
import math
import jax
import jax.numpy as jnp
import numpy as np
from jax import lax
from jax.sharding import PartitionSpec as P

K = 256
GRID = 61
NG = 8
steepness = 8.0
threshold = 0.3
shift_scale = 45
HIGH = lax.Precision.HIGH


def dot(form, left, right):
    return jnp.einsum(form, left, right, precision=HIGH, preferred_element_type=jnp.float32)


def waves(left, right, length):
    turns = np.mod(np.asarray(left)[:, None] * np.asarray(right)[None, :], length)
    angles = 2.0 * math.pi * turns.astype(np.float64) / length
    return (np.cos(angles), np.sin(angles))


def turned(first, second):
    return (
        first[0] * second[0] - first[1] * second[1],
        first[1] * second[0] + first[0] * second[1],
    )


def shifted_waves(count, freq, length, device, devices):
    near = np.stack(waves(np.arange(count), freq, length)).astype(np.float32)
    far = np.stack(waves(np.arange(devices) * count, freq, length)).astype(np.float32)
    far = lax.dynamic_slice_in_dim(jnp.asarray(far), device, 1, axis=1)
    return turned((far[0], far[1]), (jnp.asarray(near[0]), jnp.asarray(near[1])))


def on_device(
    devices, mask_field, target_print, source_points, source_groups, group_logits, pupil_radius
):
    rows, n = mask_field.shape
    sources = source_points.shape[0]
    coarse = 2 * K
    step = n // coarse
    cols = coarse // devices
    half = n // 2
    device = lax.axis_index("slab")
    freq = np.arange(K, dtype=np.int64) - K // 2
    order = np.concatenate([freq[freq % 2 == 0], freq[freq % 2 == 1]])
    kh = K // 2
    norming = 1.0 / (n * n)
    cos_y, sin_y = waves(np.arange(half), order, n)
    fold = [
        jnp.asarray(
            np.concatenate([t[:, p * kh : (p + 1) * kh] for t in (cos_y, sin_y)], 1), jnp.float32
        )
        for p in (0, 1)
    ]
    lag = np.mod(np.arange(n)[None, :] - step * np.arange(coarse // 4)[:, None], n)
    kernel = np.zeros(n)
    for f in range(1, K):
        kernel += 2.0 * np.cos(2.0 * math.pi * np.mod(f * np.arange(n), n) / n)
    kernel = (kernel + 1.0) / coarse
    quarter = lax.optimization_barrier(jnp.asarray(kernel[lag], jnp.float32))
    up = jnp.concatenate([jnp.roll(quarter, i * (n // 4), axis=1) for i in range(4)], 0)
    cos_c, sin_c = waves(freq, np.arange(coarse), coarse)
    wave_x = jnp.asarray(np.concatenate([cos_c, sin_c], 1), jnp.float32)
    loc_c, loc_s = shifted_waves(rows, freq, n, device, devices)
    loc = jnp.concatenate([loc_c, loc_s], 1)
    a, b = shifted_waves(cols, order, coarse, device, devices)
    lift = jnp.concatenate([jnp.concatenate([a, -b], 1), jnp.concatenate([b, a], 1)], 0)
    cutoff = pupil_radius[0]
    shifted = (source_points - GRID // 2) * cutoff // shift_scale
    first = jnp.asarray(freq, jnp.int32)[None, None, :] + shifted[:, 0, None, None]
    second = jnp.asarray(order, jnp.int32)[None, :, None] + shifted[:, 1, None, None]
    passed = first * first + second * second <= cutoff * cutoff
    near, away = (mask_field[:, :half], mask_field[:, half:])
    even = dot("xy,yq->xq", near + away, fold[0])
    odd = dot("xy,yq->xq", near - away, fold[1])
    part_c = jnp.concatenate([even[:, :kh], odd[:, :kh]], 1)
    part_s = jnp.concatenate([even[:, kh:], odd[:, kh:]], 1)
    spec = dot("xq,xk->qk", jnp.concatenate([part_c, part_s], 1), loc)
    band = jnp.concatenate([spec[:K, :K] - spec[K:, K:], -(spec[:K, K:] + spec[K:, :K])], 0)
    band = lax.psum(band, "slab").reshape(2, K, K)
    kept = jnp.where(passed[:, None], band[None], 0.0).reshape(sources, 2 * K, K)
    wide = dot("aq,sqk->sak", lift, kept)
    both = dot("ak,kx->ax", wide.reshape(sources * 2 * cols, K), wave_x)
    both = both.reshape(sources, 2, cols, 2 * coarse)
    field_re = (both[:, 0, :, :coarse] - both[:, 1, :, coarse:]) * norming
    field_im = (both[:, 0, :, coarse:] + both[:, 1, :, :coarse]) * norming
    bright = field_re * field_re + field_im * field_im
    onehot = (source_groups[:, None] == jnp.arange(NG, dtype=jnp.int32)[None, :]).astype(
        jnp.float32
    )
    weights = jnp.exp(jnp.sum(onehot * group_logits[None, :], 1))
    total = jnp.sum(weights)
    share = weights / total
    image = jnp.sum(share[:, None, None] * bright, 0)
    tall = dot("cm,mx->cx", image, up)
    tall = lax.all_to_all(tall, "slab", 1, 0, tiled=True)
    intensity = dot("cx,cy->xy", tall, up)
    resist = jax.nn.sigmoid(steepness * (intensity - threshold))
    misfit = resist - target_print.astype(jnp.float32)
    slope = 2.0 * steepness * misfit * resist * (1.0 - resist)
    squares = jnp.sum(misfit * misfit)
    down = dot("xy,cy->cx", slope, up)
    down = lax.all_to_all(down, "slab", 0, 1, tiled=True)
    pull = dot("cx,mx->cm", down, up)
    per_source = jnp.sum(bright * pull[None], (1, 2))
    sums = lax.psum(jnp.concatenate([per_source, squares[None]]), "slab")
    per_source, squares = (sums[:-1], sums[-1])
    loss_value = (squares * norming).reshape(1)
    against = jnp.sum(share * per_source)
    source_pull = share * (per_source - against)
    group_grad = jnp.sum(onehot * source_pull[:, None], 0) * norming
    factor = 2.0 * norming * share[:, None, None] * pull[None]
    back = jnp.stack([factor * field_re, factor * field_im], 1)
    low = dot("ax,kx->ak", back.reshape(sources * 2 * cols, coarse), wave_x[:, :coarse])
    lows = dot("ax,kx->ak", back.reshape(sources * 2 * cols, coarse), wave_x[:, coarse:])
    low = low.reshape(sources, 2, cols, K)
    lows = lows.reshape(sources, 2, cols, K)
    settle = jnp.concatenate([low[:, 0] + lows[:, 1], low[:, 1] - lows[:, 0]], 1)
    settle = dot("aq,sak->sqk", lift, settle).reshape(sources, 2, K, K)
    grad_band = jnp.sum(jnp.where(passed[:, None], settle, 0.0), 0)
    grad_band = lax.psum(grad_band.reshape(2 * K, K), "slab")
    loc_c2 = jnp.concatenate([loc_c, loc_s], 0)
    spread = dot("tk,qk->tq", loc_c2, grad_band)
    spread_re = spread[:rows, :K] - spread[rows:, K:]
    spread_im = spread[:rows, K:] + spread[rows:, :K]
    even = dot("xq,yq->xy", jnp.concatenate([spread_re[:, :kh], -spread_im[:, :kh]], 1), fold[0])
    odd = dot("xq,yq->xy", jnp.concatenate([spread_re[:, kh:], -spread_im[:, kh:]], 1), fold[1])
    mask_grad = jnp.concatenate([even + odd, even - odd], 1)
    return (loss_value, mask_grad, group_grad)


def solution(mesh):
    in_specs = (
        P(("clip", "slab"), None),
        P(("clip", "slab"), None),
        P("clip", None),
        P("clip"),
        P("clip"),
        P("clip"),
    )
    out_specs = (P("clip"), P(("clip", "slab"), None), P("clip"))
    return jax.shard_map(
        functools.partial(on_device, mesh.shape["slab"]),
        mesh=mesh,
        in_specs=in_specs,
        out_specs=out_specs,
        check_vma=False,
    )
```

profile of v0, /device:TPU:0, one launch (start us, length us, event | category | flops | bytes accessed | tf_op | source)
XLA Modules:
  0.0 301.4 jit_solution(10782398670884139103)
XLA Ops:
  7.2 0.0 all-reduce.3.cloned.1.call-start
  7.2 0.0 copy-start.1
  7.2 2.0 fusion.31
  9.3 2.0 fusion.29
  11.3 0.8 constant_dynamic-slice_fusion
  12.1 1.0 multiply_subtract_fusion
  13.1 0.6 fusion.41
  13.7 0.1 slice_subtract_fusion.2
  13.8 0.0 copy-start.13
  13.8 0.0 copy-start.14
  13.8 0.0 copy-start.12
  13.8 0.0 copy-start.10
  13.8 0.0 copy-start.11
  13.8 0.9 pad_maximum_fusion.4
  14.7 0.0 all-reduce.3.cloned.1.call-update
  14.7 0.0 all-reduce.5.cloned.1.call-start
  14.8 0.9 fusion.73
  15.6 0.9 fusion.75
  16.5 0.1 fusion.74
  17.2 0.1 select_reduce_fusion.1
  17.3 0.6 exponential_reduce_fusion
  18.0 0.1 add_multiply_fusion
  18.1 0.9 add_compare_fusion
  18.9 5.2 %maximum_maximum_fusion = f32[512,2048]{0,1:T(8,128)} fusion(f32[128,512]{0,1:T(8,128)} %get-tuple-element.12, f32[128,1536]{0,1:T(8,128)S(1)} %get-tuple-element.14, f32[128,1024]{0,1:T(8,128)} %get-tuple-element.16, f32[128,1024]{0,1:T(8,128)S(1)} %get-tuple-element.15, f32[128,1536]{0,1:T(8,128)S(1)} %get-tuple-element.13, ...), kind=kLoop, calls=%fused_computation.4 | loop fusion | flops 6291456 | bytes 8388608 | tf_op jit(solution)/shard_map/concatenate | solution.py:69
  24.1 0.7 broadcast_multiply_fusion.1
  24.8 1.0 broadcast_in_dim.28
  25.8 0.0 copy-start.3
  25.8 4.3 %copy.46 = pred[16,512,256]{1,2,0:T(32,128)(4,1)S(1)} copy(pred[16,512,256]{2,1,0:T(32,128)(4,1)S(1)} %bitcast.90) | data formatting | bytes 4194304 | tf_op jit(solution)/shard_map/jit(_where)/broadcast_in_dim | solution.py:89
  30.2 78.1 %all-reduce.3.cloned.1.call-done = f32[512,256]{1,0:T(8,128)} async-done(((f32[512,256]{1,0:T(8,128)}), f32[512,256]{1,0:T(8,128)}) %all-reduce.3.cloned.1.call-update) | async-done | bytes 524304 | tf_op jit(solution)/shard_map/psum | solution.py:88
  108.3 2.0 copy.45
  110.3 5.4 %fusion.1 = f32[16,256,64]{1,2,0:T(8,128)S(1)} fusion(pred[16,512,256]{1,2,0:T(32,128)(4,1)S(1)} %copy.46, f32[512,256]{0,1:T(8,128)} %copy.45, f32[32,256]{1,0:T(8,128)S(1)} %get-tuple-element.27, f32[32,256]{1,0:T(8,128)S(1)} %get-tuple-element.26, f32[32,256]{1,0:T(8,128)S(1)} %get-tuple-element.25), kind=kOutput, calls=%fused_computation.2 | convolution fusion | flops 807501824 | bytes 3768320 | tf_op jit(solution)/shard_map/aq,sqk->sak/dot_general | solution.py:19
  115.7 1.9 fusion.78
  117.6 0.0 copy-start.2
  117.6 0.5 fusion.17
  118.1 2.0 fusion.60
  120.2 15.0 %all_to_all.35 = f32[32,16,128]{2,0,1:T(8,128)S(1)} all-to-all(f32[32,16,128]{2,0,1:T(8,128)S(1)} %fusion.60), channel_id=1, replica_groups=mesh['clip'=2,'slab'=16] {'slab'}, dimensions={1} | all-to-all | bytes 524288 | tf_op jit(solution)/shard_map/all_to_all | solution.py:104
  135.1 2.8 multiply_reduce_fusion
  137.9 3.5 %fusion.19 = f32[512,128]{1,0:T(8,128)S(1)} fusion(f32[512,2048]{0,1:T(8,128)S(1)} %copy-done, f32[128,2048]{1,0:T(8,128)S(1)} %get-tuple-element.35, s32[128,2048]{1,0:T(8,128)S(1)} %copy-done.2), kind=kOutput, calls=%fused_computation.34 | convolution fusion | flops 806879232 | bytes 6553600 | tf_op jit(solution)/shard_map/xy,cy->cx/dot_general | solution.py:19
  141.4 12.7 %all_to_all.36 = f32[16,32,128]{2,1,0:T(8,128)S(1)} all-to-all(f32[16,32,128]{2,1,0:T(8,128)S(1)} %bitcast.91), channel_id=1, replica_groups=mesh['clip'=2,'slab'=16] {'slab'}, dimensions={0} | all-to-all | bytes 524288 | tf_op jit(solution)/shard_map/all_to_all | solution.py:111
  154.1 1.5 fusion.37
  155.5 0.4 fusion.18
  156.0 0.6 multiply_multiply_fusion.1
  156.6 0.4 copy-done.6
  157.0 1.0 fusion.10
  158.1 1.0 fusion.11
  159.1 0.7 pad_maximum_fusion.5
  159.8 0.1 fusion.24
  159.9 0.9 fusion.26
  160.8 31.1 %psum.22 = f32[17]{0:T(128)S(1)} all-reduce(f32[17]{0:T(128)S(1)} %pad_maximum_fusion.5), channel_id=1, replica_groups=mesh['clip'=2,'slab'=16] {'slab'}, use_global_device_ids=true, to_apply=%region_6.7 | all-reduce | flops 17 | bytes 136 | tf_op jit(solution)/shard_map/psum | solution.py:114
  191.8 0.6 multiply_reduce_fusion.1
  192.4 0.6 subtract_multiply_fusion
  193.1 0.0 copy-start.4
  193.1 5.9 %fusion = f32[512,256]{0,1:T(8,128)} fusion(pred[16,512,256]{1,2,0:T(32,128)(4,1)S(1)} %copy.46, f32[16,32,256]{2,1,0:T(8,128)S(1)} %fusion.24, f32[16,32,256]{2,1,0:T(8,128)} %fusion.26, f32[32,256]{1,0:T(8,128)S(1)} %get-tuple-element.27, f32[32,256]{1,0:T(8,128)S(1)} %get-tuple-element.26, f32[32,256]{1,0:T(8,128)S(1)} %get-tuple-element.25), kind=kOutput, calls=%fused_computation.1 | convolution fusion | flops 809730048 | bytes 3768320 | tf_op jit(solution)/shard_map/aq,sak->sqk/dot_general | solution.py:19
  199.0 0.0 all-reduce.5.cloned.1.call-update
  199.0 0.1 select_reduce_fusion
  199.2 0.6 slice.161
  200.4 0.5 broadcast_multiply_fusion
  200.9 86.3 %all-reduce.5.cloned.1.call-done = f32[512,256]{0,1:T(8,128)} async-done(((f32[512,256]{0,1:T(8,128)}), f32[512,256]{0,1:T(8,128)}) %all-reduce.5.cloned.1.call-update) | async-done | bytes 524304 | tf_op jit(solution)/shard_map/psum | solution.py:129
  287.2 1.4 fusion.52
  288.7 1.4 fusion.56
  290.1 1.4 fusion.58
  291.5 0.4 convolution_add_fusion.1
  291.9 0.4 fusion.72
  292.4 1.0 pad_maximum_fusion.3
  (25 shorter events, 0.1 us)
Async XLA Ops:
  7.2 101.1 %all-reduce.3.cloned.1.call-start = ((), (), s32[]{:S(2)}) async-start(), calls=%async_computation.2 | async-start | bytes 1048576 | tf_op jit(solution)/shard_map/psum | solution.py:88
  7.2 7.5 %copy-start.1 = (f32[128,2048]{0,1:T(8,128)S(1)}, f32[128,2048]{0,1:T(8,128)}, u32[]{:S(2)}) copy-start(f32[128,2048]{0,1:T(8,128)} %constant.68.clone) | copy-start | bytes 3145732
  13.8 3.5 %copy-start.13 = (f32[8]{0:T(128)S(1)}, f32[8]{0:T(128)}, u32[]{:S(2)}) copy-start(f32[8]{0:T(128)} %param.22) | copy-start | bytes 100
  13.8 3.5 %copy-start.14 = (s32[16]{0:T(128)S(1)}, s32[16]{0:T(128)}, u32[]{:S(2)}) copy-start(s32[16]{0:T(128)} %param.21) | copy-start | bytes 196
  13.8 4.2 %copy-start.12 = (s32[16,2]{0,1:T(2,128)S(1)}, s32[16,2]{0,1:T(2,128)}, u32[]{:S(2)}) copy-start(s32[16,2]{0,1:T(2,128)} %param.20) | copy-start | bytes 388
  13.8 4.2 %copy-start.10 = (s32[256]{0:T(256)S(1)}, s32[256]{0:T(256)}, u32[]{:S(2)}) copy-start(s32[256]{0:T(256)} %constant.77.clone) | copy-start | bytes 3076
  13.8 4.2 %copy-start.11 = (s32[256]{0:T(256)S(1)}, s32[256]{0:T(256)}, u32[]{:S(2)}) copy-start(s32[256]{0:T(256)} %constant.76.clone) | copy-start | bytes 3076
  14.7 272.5 %all-reduce.5.cloned.1.call-start = ((), (), s32[]{:S(2)}) async-start(), calls=%async_computation.3 | async-start | bytes 1048576 | tf_op jit(solution)/shard_map/psum | solution.py:129
  24.1 6.0 %copy-start.8 = (f32[32,256]{1,0:T(8,128)S(1)}, f32[32,256]{1,0:T(8,128)}, u32[]{:S(2)}) copy-start(f32[32,256]{1,0:T(8,128)} %constant.75.clone) | copy-start | bytes 98308
  24.1 6.0 %copy-start.9 = (f32[32,256]{1,0:T(8,128)S(1)}, f32[32,256]{1,0:T(8,128)}, u32[]{:S(2)}) copy-start(f32[32,256]{1,0:T(8,128)} %constant.74.clone) | copy-start | bytes 98308
  25.8 89.9 %copy-start.3 = (f32[256,1024,1,1]{1,0,3,2:T(8,128)S(1)}, f32[256,1024,1,1]{1,0,3,2:T(8,128)}, u32[]{:S(2)}) copy-start(f32[256,1024,1,1]{1,0,3,2:T(8,128)} %constant.85) | copy-start | bytes 3145732
  115.7 2.4 copy-start
  117.6 17.6 %copy-start.2 = (s32[128,2048]{1,0:T(8,128)S(1)}, s32[128,2048]{1,0:T(8,128)}, u32[]{:S(2)}) copy-start(s32[128,2048]{1,0:T(8,128)} %param.19) | copy-start | bytes 3145732
  156.0 1.0 copy-start.6
  156.0 2.1 copy-start.5
  193.1 98.4 %copy-start.4 = (f32[1024,128]{1,0:T(8,128)S(1)}, f32[1024,128]{1,0:T(8,128)}, u32[]{:S(2)}) copy-start(f32[1024,128]{1,0:T(8,128)} %constant.84) | copy-start | bytes 1572868
  199.0 92.9 %copy-start.7 = (f32[1024,128]{1,0:T(8,128)S(1)}, f32[1024,128]{1,0:T(8,128)}, u32[]{:S(2)}) copy-start(f32[1024,128]{1,0:T(8,128)} %constant.82) | copy-start | bytes 1572868
Sparse Core Ops, SparseCore 0:
  14.8 93.4 all-reduce.2
  199.2 87.9 all-reduce.4
where the time goes:
time: 302 us; the launch traced here: 301 us
  waiting for transfers between devices  164 us (54%)
  blocking collectives  58.7 us (19%)
  matrix products  34.6 us (11%)
  between operations  16.9 us (6%)
  other arithmetic  15.6 us (5%)
  local copies, waits for them, and re-layouts  11.1 us (4%)
    psum x1, waiting for transfers between devices, on_device(): grad_band = lax.psum(grad_band.reshape(2 * K, K), 'slab')  86.3 us
    psum x1, waiting for transfers between devices, on_device(): band = lax.psum(band, 'slab').reshape(2, K, K)  78.1 us
    dot_general x17, matrix products, dot(): jnp.einsum(form, left, right, precision=HIGH, preferred_element_type=jnp....  34.6 us
    psum x1, blocking collectives, on_device(): sums = lax.psum(jnp.concatenate([per_source, squares[None]]), 'slab')  31.1 us
    all_to_all x1, blocking collectives, on_device(): tall = lax.all_to_all(tall, 'slab', 1, 0, tiled=True)  15 us
    all_to_all x1, blocking collectives, on_device(): down = lax.all_to_all(down, 'slab', 0, 1, tiled=True)  12.7 us
  transfers between devices with their start and end apart: 2, of which 2 were waited for; matrix products, arithmetic and copies ran while one was open for 5% of the time, Pallas kernels for 0%

commit v1 on v0

--- a/solution.py
+++ b/solution.py
@@ -85,7 +85,7 @@
     part_s = jnp.concatenate([even[:, kh:], odd[:, kh:]], 1)
     spec = dot("xq,xk->qk", jnp.concatenate([part_c, part_s], 1), loc)
     band = jnp.concatenate([spec[:K, :K] - spec[K:, K:], -(spec[:K, K:] + spec[K:, :K])], 0)
-    band = lax.psum(band, "slab").reshape(2, K, K)
+    band = jnp.sum(lax.all_gather(band, "slab"), axis=0).reshape(2, K, K)
     kept = jnp.where(passed[:, None], band[None], 0.0).reshape(sources, 2 * K, K)
     wide = dot("aq,sqk->sak", lift, kept)
     both = dot("ak,kx->ax", wide.reshape(sources * 2 * cols, K), wave_x)

time: 302 us -> 285 us (0.944)
  waiting for transfers between devices: 164 us -> 150 us
  other arithmetic: 15.6 us -> 19.5 us
  local copies, waits for them, and re-layouts: 11.1 us -> 7.51 us
    psum x1 -> x0, waiting for transfers between devices: 78.1 us -> none  [on_device(): band = lax.psum(band, 'slab').reshape(2, K, K)]
    all_gather x0 -> x1, waiting for transfers between devices: none -> 63.4 us  [on_device(): band = jnp.sum(lax.all_gather(band, 'slab'), axis=0).reshape(2, K, K)]
    reduce_sum x0 -> x1, other arithmetic: none -> 3.98 us  [on_device(): band = jnp.sum(lax.all_gather(band, 'slab'), axis=0).reshape(2, K, K)]
where the time goes in v1:
time: 285 us; the launch traced here: 284 us
  waiting for transfers between devices  150 us (53%)
  blocking collectives  56.9 us (20%)
  matrix products  33.5 us (12%)
  other arithmetic  19.5 us (7%)
  between operations  16.9 us (6%)
  local copies, waits for them, and re-layouts  7.51 us (3%)
    psum x1, waiting for transfers between devices, on_device(): grad_band = lax.psum(grad_band.reshape(2 * K, K), 'slab')  86.2 us
    all_gather x1, waiting for transfers between devices, on_device(): band = jnp.sum(lax.all_gather(band, 'slab'), axis=0).reshape(2, K, K)  63.4 us
    dot_general x17, matrix products, dot(): jnp.einsum(form, left, right, precision=HIGH, preferred_element_type=jnp....  33.5 us
    psum x1, blocking collectives, on_device(): sums = lax.psum(jnp.concatenate([per_source, squares[None]]), 'slab')  31.1 us
    all_to_all x1, blocking collectives, on_device(): tall = lax.all_to_all(tall, 'slab', 1, 0, tiled=True)  13.1 us
    all_to_all x1, blocking collectives, on_device(): down = lax.all_to_all(down, 'slab', 0, 1, tiled=True)  12.7 us
  transfers between devices with their start and end apart: 2, of which 2 were waited for; matrix products, arithmetic and copies ran while one was open for 5% of the time, Pallas kernels for 0%

profile of v1, /device:TPU:0, one launch (start us, length us, event | category | flops | bytes accessed | tf_op | source)
XLA Modules:
  0.0 284.0 jit_solution(4353629226123373130)
XLA Ops:
  7.2 0.0 all-gather.3.cloned.1.call-start
  7.2 0.0 copy-start.12
  7.2 0.0 copy-start.10
  7.2 0.0 copy-start.11
  7.2 2.0 fusion.31
  9.2 2.0 fusion.29
  11.2 0.8 constant_dynamic-slice_fusion
  12.0 1.0 multiply_subtract_fusion
  13.0 0.6 fusion.41
  13.6 0.1 slice_subtract_fusion.2
  13.7 0.8 pad_maximum_fusion.4
  14.5 0.0 all-gather.3.cloned.1.call-update
  14.6 0.0 all-reduce.2.cloned.1.call-start
  15.3 0.1 add_multiply_fusion
  15.4 0.0 copy-start.9
  15.4 0.0 copy-start.1
  15.4 0.9 add_compare_fusion
  16.3 0.9 broadcast_in_dim.28
  17.3 4.3 %copy.44 = pred[16,512,256]{1,2,0:T(32,128)(4,1)S(1)} copy(pred[16,512,256]{2,1,0:T(32,128)(4,1)S(1)} %bitcast.92) | data formatting | bytes 4194304 | tf_op jit(solution)/shard_map/jit(_where)/broadcast_in_dim | solution.py:89
  21.6 0.0 copy-done.13
  21.6 0.1 select_reduce_fusion.1
  21.7 0.6 exponential_reduce_fusion
  22.3 0.7 broadcast_multiply_fusion.1
  23.0 0.1 fusion.75
  23.1 0.1 fusion.74
  23.2 5.1 %maximum_maximum_fusion = f32[512,2048]{0,1:T(8,128)} fusion(f32[128,512]{0,1:T(8,128)S(1)} %get-tuple-element.12, f32[128,1536]{0,1:T(8,128)S(1)} %get-tuple-element.14, f32[128,1024]{0,1:T(8,128)S(1)} %get-tuple-element.16, f32[128,1024]{0,1:T(8,128)S(1)} %get-tuple-element.15, f32[128,1536]{0,1:T(8,128)S(1)} %get-tuple-element.13, ...), kind=kLoop, calls=%fused_computation.4 | loop fusion | flops 6291456 | bytes 8388608 | tf_op jit(solution)/shard_map/concatenate | solution.py:69
  28.3 63.4 %all-gather.3.cloned.1.call-done = f32[8192,256]{1,0:T(8,128)} async-done(((f32[512,256]{1,0:T(8,128)}), f32[8192,256]{1,0:T(8,128)}) %all-gather.3.cloned.1.call-update) | async-done | bytes 8388624 | tf_op jit(solution)/shard_map/all_gather | solution.py:88
  91.7 4.0 %reduce_sum.81 = f32[512,256]{1,0:T(8,128)S(1)} reduce(f32[16,512,256]{2,1,0:T(8,128)} %bitcast.91, f32[]{:T(128)} %constant.58.clone.1), dimensions={0}, to_apply=%region_0.1 | reduce | flops 1966080 | bytes 8912900 | tf_op jit(solution)/shard_map/reduce_sum | solution.py:88
  95.7 0.2 copy.43
  95.9 0.0 copy-start.3
  95.9 4.3 %fusion.1 = f32[16,256,64]{1,2,0:T(8,128)S(1)} fusion(pred[16,512,256]{1,2,0:T(32,128)(4,1)S(1)} %copy.44, f32[512,256]{0,1:T(8,128)S(1)} %copy.43, f32[32,256]{1,0:T(8,128)S(1)} %get-tuple-element.27, f32[32,256]{1,0:T(8,128)S(1)} %get-tuple-element.26, f32[32,256]{1,0:T(8,128)S(1)} %get-tuple-element.25), kind=kOutput, calls=%fused_computation.2 | convolution fusion | flops 807501824 | bytes 3768320 | tf_op jit(solution)/shard_map/aq,sqk->sak/dot_general | solution.py:19
  100.3 1.9 fusion.78
  102.2 0.0 copy-start.2
  102.2 0.5 fusion.17
  102.7 2.0 fusion.60
  104.7 13.1 %all_to_all.35 = f32[32,16,128]{2,0,1:T(8,128)S(1)} all-to-all(f32[32,16,128]{2,0,1:T(8,128)S(1)} %fusion.60), channel_id=1, replica_groups=mesh['clip'=2,'slab'=16] {'slab'}, dimensions={1} | all-to-all | bytes 524288 | tf_op jit(solution)/shard_map/all_to_all | solution.py:104
  117.9 2.8 multiply_reduce_fusion
  120.6 3.5 %fusion.19 = f32[512,128]{1,0:T(8,128)S(1)} fusion(f32[512,2048]{0,1:T(8,128)S(1)} %copy-done, f32[128,2048]{1,0:T(8,128)S(1)} %get-tuple-element.35, s32[128,2048]{1,0:T(8,128)S(1)} %copy-done.2), kind=kOutput, calls=%fused_computation.34 | convolution fusion | flops 806879232 | bytes 6553600 | tf_op jit(solution)/shard_map/xy,cy->cx/dot_general | solution.py:19
  124.1 12.7 %all_to_all.36 = f32[16,32,128]{2,1,0:T(8,128)S(1)} all-to-all(f32[16,32,128]{2,1,0:T(8,128)S(1)} %bitcast.93), channel_id=1, replica_groups=mesh['clip'=2,'slab'=16] {'slab'}, dimensions={0} | all-to-all | bytes 524288 | tf_op jit(solution)/shard_map/all_to_all | solution.py:111
  136.8 1.5 fusion.37
  138.2 0.4 fusion.18
  138.7 0.6 multiply_multiply_fusion.1
  139.3 0.4 copy-done.6
  139.7 1.0 fusion.10
  140.8 1.0 fusion.11
  141.8 0.7 pad_maximum_fusion.5
  142.5 0.1 fusion.24
  142.6 0.9 fusion.26
  143.5 31.1 %psum.14 = f32[17]{0:T(128)S(1)} all-reduce(f32[17]{0:T(128)S(1)} %pad_maximum_fusion.5), channel_id=1, replica_groups=mesh['clip'=2,'slab'=16] {'slab'}, use_global_device_ids=true, to_apply=%region_6.7 | all-reduce | flops 17 | bytes 136 | tf_op jit(solution)/shard_map/psum | solution.py:114
  174.5 0.6 multiply_reduce_fusion.1
  175.1 0.6 subtract_multiply_fusion
  175.8 0.0 copy-start.4
  175.8 5.9 %fusion = f32[512,256]{0,1:T(8,128)} fusion(pred[16,512,256]{1,2,0:T(32,128)(4,1)S(1)} %copy.44, f32[16,32,256]{2,1,0:T(8,128)S(1)} %fusion.24, f32[16,32,256]{2,1,0:T(8,128)} %fusion.26, f32[32,256]{1,0:T(8,128)S(1)} %get-tuple-element.27, f32[32,256]{1,0:T(8,128)S(1)} %get-tuple-element.26, f32[32,256]{1,0:T(8,128)S(1)} %get-tuple-element.25), kind=kOutput, calls=%fused_computation.1 | convolution fusion | flops 809730048 | bytes 3768320 | tf_op jit(solution)/shard_map/aq,sak->sqk/dot_general | solution.py:19
  181.7 0.0 all-reduce.2.cloned.1.call-update
  181.8 0.1 select_reduce_fusion
  181.9 0.6 slice.161
  183.1 0.5 broadcast_multiply_fusion
  183.6 86.2 %all-reduce.2.cloned.1.call-done = f32[512,256]{0,1:T(8,128)} async-done(((f32[512,256]{0,1:T(8,128)}), f32[512,256]{0,1:T(8,128)}) %all-reduce.2.cloned.1.call-update) | async-done | bytes 524304 | tf_op jit(solution)/shard_map/psum | solution.py:129
  269.8 1.4 fusion.52
  271.3 1.4 fusion.56
  272.7 1.4 fusion.58
  274.1 0.4 convolution_add_fusion.1
  274.6 0.4 fusion.72
  275.0 1.0 pad_maximum_fusion.3
  (26 shorter events, 0.2 us)
Async XLA Ops:
  7.2 84.6 %all-gather.3.cloned.1.call-start = ((), (), s32[]{:S(2)}) async-start(), calls=%async_computation.3 | async-start | bytes 8912896 | tf_op jit(solution)/shard_map/all_gather | solution.py:88
  7.2 8.0 %copy-start.12 = (s32[16,2]{0,1:T(2,128)S(1)}, s32[16,2]{0,1:T(2,128)}, u32[]{:S(2)}) copy-start(s32[16,2]{0,1:T(2,128)} %param.20) | copy-start | bytes 388
  7.2 8.1 %copy-start.10 = (s32[256]{0:T(256)S(1)}, s32[256]{0:T(256)}, u32[]{:S(2)}) copy-start(s32[256]{0:T(256)} %constant.77.clone) | copy-start | bytes 3076
  7.2 8.1 %copy-start.11 = (s32[256]{0:T(256)S(1)}, s32[256]{0:T(256)}, u32[]{:S(2)}) copy-start(s32[256]{0:T(256)} %constant.76.clone) | copy-start | bytes 3076
  14.6 255.3 %all-reduce.2.cloned.1.call-start = ((), (), s32[]{:S(2)}) async-start(), calls=%async_computation.2 | async-start | bytes 1048576 | tf_op jit(solution)/shard_map/psum | solution.py:129
  15.4 6.2 %copy-start.13 = (f32[8]{0:T(128)S(1)}, f32[8]{0:T(128)}, u32[]{:S(2)}) copy-start(f32[8]{0:T(128)} %param.22) | copy-start | bytes 100
  15.4 6.2 %copy-start.14 = (s32[16]{0:T(128)S(1)}, s32[16]{0:T(128)}, u32[]{:S(2)}) copy-start(s32[16]{0:T(128)} %param.21) | copy-start | bytes 196
  15.4 7.6 %copy-start.8 = (f32[32,256]{1,0:T(8,128)S(1)}, f32[32,256]{1,0:T(8,128)}, u32[]{:S(2)}) copy-start(f32[32,256]{1,0:T(8,128)} %constant.75.clone) | copy-start | bytes 98308
  15.4 7.6 %copy-start.9 = (f32[32,256]{1,0:T(8,128)S(1)}, f32[32,256]{1,0:T(8,128)}, u32[]{:S(2)}) copy-start(f32[32,256]{1,0:T(8,128)} %constant.74.clone) | copy-start | bytes 98308
  15.4 7.6 %copy-start.1 = (f32[128,2048]{0,1:T(8,128)S(1)}, f32[128,2048]{0,1:T(8,128)}, u32[]{:S(2)}) copy-start(f32[128,2048]{0,1:T(8,128)} %constant.68.clone) | copy-start | bytes 3145732
  95.9 4.3 %copy-start.3 = (f32[256,1024,1,1]{1,0,3,2:T(8,128)S(1)}, f32[256,1024,1,1]{1,0,3,2:T(8,128)}, u32[]{:S(2)}) copy-start(f32[256,1024,1,1]{1,0,3,2:T(8,128)} %constant.85) | copy-start | bytes 3145732
  100.3 2.5 copy-start
  102.2 15.7 %copy-start.2 = (s32[128,2048]{1,0:T(8,128)S(1)}, s32[128,2048]{1,0:T(8,128)}, u32[]{:S(2)}) copy-start(s32[128,2048]{1,0:T(8,128)} %param.19) | copy-start | bytes 3145732
  138.7 1.0 copy-start.6
  138.7 2.1 copy-start.5
  175.8 98.3 %copy-start.4 = (f32[1024,128]{1,0:T(8,128)S(1)}, f32[1024,128]{1,0:T(8,128)}, u32[]{:S(2)}) copy-start(f32[1024,128]{1,0:T(8,128)} %constant.84) | copy-start | bytes 1572868
  181.7 92.8 %copy-start.7 = (f32[1024,128]{1,0:T(8,128)S(1)}, f32[1024,128]{1,0:T(8,128)}, u32[]{:S(2)}) copy-start(f32[1024,128]{1,0:T(8,128)} %constant.82) | copy-start | bytes 1572868
Sparse Core Ops, SparseCore 0:
  14.7 77.0 all-gather.2
  181.9 87.9 all-reduce.1
